TPU v7x, 32 devices: a whole 2x2x4 slice. The times are simulated.
32 devices in a mesh: shard: 4 (over x, core), seq: 8 (over z, y).
Axes of the slice: x: 2, y: 2, z: 4, core: 2. Of those that a mesh axis runs over, the one named last changes fastest.
Arguments:
- hidden: bfloat16 [16384, 1536], P(('shard', 'seq')), may hold values from -6 to 6
- cotangent: bfloat16 [16384, 1536], P(('shard', 'seq')), may hold values from -6 to 6
- seg_ids: int32 [16384], replicated, may hold values from 0 to 7, never falling along the last dimension, each value on 1 to 4096 neighbouring positions
- norm_gain: bfloat16 [1536], P('shard'), may hold values from 0.5 to 1.5
- in_weight: bfloat16 [1536, 6448], P('shard'), may hold values from -0.15625 to 0.15625
- conv_weight: bfloat16 [4, 3328], P(None, 'shard'), may hold values from -3 to 3
- conv_bias: bfloat16 [3328], P('shard'), may hold values from -3 to 3
- dt_bias: bfloat16 [48], replicated, may hold values from -8 to -2
- a_log: bfloat16 [48], replicated, may hold values from 0 to 2.6875
- d_skip: bfloat16 [48], replicated, may hold values from 0.5 to 1.5
- out_gain: bfloat16 [3072], P('shard'), may hold values from 0.5 to 1.5
- out_weight: bfloat16 [3072, 1536], P('shard'), may hold values from -0.109375 to 0.109375
Outputs:
- block_out: bfloat16 [16384, 1536], P(('shard', 'seq'))
- grad_hidden: float32 [16384, 1536], P(('shard', 'seq'))
- grad_norm_gain: float32 [1536], P(('shard', 'seq'))
- grad_in_weight: float32 [1536, 6448], P(('shard', 'seq'))
- grad_conv_weight: float32 [4, 3328], P(None, ('shard', 'seq'))
- grad_conv_bias: float32 [3328], P(('shard', 'seq'))
- grad_dt_bias: float32 [48], replicated
- grad_a_log: float32 [48], replicated
- grad_d_skip: float32 [48], replicated
- grad_out_gain: float32 [3072], P(('shard', 'seq'))
- grad_out_weight: float32 [3072, 1536], P(('shard', 'seq'))
Inputs may be any that keep to these rules, and one draw needn't show every extreme that they name: seg_ids never falls along the tokens; every value occurs; each document holds 1 to 4096 tokens and one holds exactly 4096.
All inputs are finite; a program needn't handle non-finite values.
Results may differ from a plain program's by a relative error of at most 0.02.
Values may be sent and summed in bfloat16 or wider, within the bound.
No kernel may reach another device: no remote copies, remote signals or barrier semaphores. Data moves between devices by JAX's collectives and lax.ppermute only.
A program may use at most 384 MiB of HBM per device.

v0:
```python
import jax
import jax.numpy as jnp
from jax import lax
from jax.sharding import PartitionSpec as P

HEAD_DIM = 64
CONV = 4
BLOCK = 256
HIGH = lax.Precision.HIGHEST
EPS = 1e-05


def from_behind(value, axis, steps):
    count = lax.axis_size(axis)
    initial, last = (max(0, -steps), min(count, count - steps))
    return lax.ppermute(value, axis, [(source, source + steps) for source in range(initial, last)])


def prefix(array, axis, join, neutral, backward):
    count = lax.axis_size(axis)
    place = lax.axis_index(axis)
    ahead = count - 1 - place if backward else place
    gathered = jax.tree.map(
        lambda a, kind: lax.all_gather(a.astype(kind), axis), array, (jnp.bfloat16, jnp.bfloat16)
    )
    state = jax.tree.map(lambda a, e: jnp.zeros_like(a) + jnp.asarray(e, a.dtype), array, neutral)

    def one(step, state):
        source = count - 1 - step if backward else step
        return join(
            state,
            jax.tree.map(
                lambda a, own: lax.dynamic_index_in_dim(a, source, 0, False).astype(own.dtype),
                gathered,
                array,
            ),
        )

    return lax.fori_loop(0, ahead, one, state)


def token_norm(values, gain):
    scale = lax.rsqrt(jnp.mean(values * values, axis=1, keepdims=True) + EPS)
    return values * scale * gain[None, :]


def gate_norm(mixer_out, gate_z, gain):
    gated = mixer_out * jax.nn.silu(gate_z)
    scale = lax.rsqrt(jnp.mean(gated * gated, axis=1, keepdims=True) + EPS)
    return gated * scale * gain[None, :]


def chain_pairs(earlier, later):
    return (earlier[0] * later[0], later[0][None, :] * earlier[1] + later[1])


def causal_conv(extended, seg_ext, weight, bias, length):
    seg_here = seg_ext[CONV - 1 :]
    summed = jnp.zeros((length, extended.shape[1]), jnp.float32) + bias[None, :]
    for tap in range(CONV):
        same_doc = (seg_ext[tap : tap + length] == seg_here).astype(jnp.float32)
        summed = summed + weight[tap][None, :] * extended[tap : tap + length] * same_doc[:, None]
    return jax.nn.silu(summed)


def make_mixer(seg_ext, head_lo, channel_lo):

    def mixer(
        x_raw,
        bc_raw,
        dt_raw,
        tail_x,
        tail_bc,
        conv_x,
        bias_x,
        conv_bc,
        bias_bc,
        dt_bias,
        a_log,
        d_skip,
    ):
        length = x_raw.shape[0]
        chan_width = x_raw.shape[1]
        n_state = bc_raw.shape[1] // 2
        local_heads = (chan_width - 1) // HEAD_DIM + 2
        seg_here = seg_ext[CONV - 1 :]
        x_conv = causal_conv(jnp.concatenate([tail_x, x_raw], 0), seg_ext, conv_x, bias_x, length)
        bc_conv = causal_conv(
            jnp.concatenate([tail_bc, bc_raw], 0), seg_ext, conv_bc, bias_bc, length
        )
        b_mat = bc_conv[:, :n_state]
        c_mat = bc_conv[:, n_state:]
        step_size = jax.nn.softplus(dt_raw + dt_bias[None, :])
        log_decay = -step_size * jnp.exp(a_log)[None, :]
        padding = jnp.zeros((length, local_heads - 1), jnp.float32)
        step_local = lax.dynamic_slice_in_dim(
            jnp.concatenate([step_size, padding], 1), head_lo, local_heads, 1
        )
        decay_local = lax.dynamic_slice_in_dim(
            jnp.concatenate([log_decay, padding], 1), head_lo, local_heads, 1
        )
        skip_local = lax.dynamic_slice_in_dim(
            jnp.concatenate([d_skip, jnp.zeros((local_heads - 1,), jnp.float32)]),
            head_lo,
            local_heads,
        )
        owner = (channel_lo + jnp.arange(chan_width, dtype=jnp.int32)) // HEAD_DIM - head_lo
        select = (owner[None, :] == jnp.arange(local_heads, dtype=jnp.int32)[:, None]).astype(
            jnp.float32
        )
        x_step = x_conv * jnp.dot(step_local, select, precision=HIGH)
        n_blocks = length // BLOCK
        seg_before = seg_ext[CONV - 2 : CONV - 2 + length].reshape(n_blocks, BLOCK)[:, 0]

        def block_step(state, inputs):
            x_block, b_block, c_block, decay_block, seg_block, seg_prior = inputs
            cum_decay = jnp.cumsum(decay_block, axis=0)
            positions = jnp.arange(BLOCK, dtype=jnp.int32)
            same_doc = (seg_block[:, None] == seg_block[None, :]) & (
                positions[:, None] >= positions[None, :]
            )
            log_gap = cum_decay.T[:, :, None] - cum_decay.T[:, None, :]
            weights = jnp.exp(jnp.where(same_doc[None], log_gap, -jnp.inf))
            scores = jnp.dot(c_block, b_block.T, precision=HIGH)
            per_head = jnp.einsum("jts,sc->jtc", weights * scores[None], x_block, precision=HIGH)
            inside = jnp.sum(per_head * select[:, None, :], axis=0)
            entering = jnp.exp(cum_decay) * (seg_block == seg_prior).astype(jnp.float32)[:, None]
            enter_block = jnp.dot(entering, select, precision=HIGH)
            from_state = jnp.dot(c_block, state, precision=HIGH) * enter_block
            keep_tail = jnp.exp(
                jnp.where(
                    (seg_block == seg_block[BLOCK - 1])[:, None],
                    cum_decay[BLOCK - 1][None, :] - cum_decay,
                    -jnp.inf,
                )
            )
            tail_channels = jnp.dot(keep_tail, select, precision=HIGH)
            new_state = enter_block[BLOCK - 1][None, :] * state + jnp.dot(
                b_block.T, x_block * tail_channels, precision=HIGH
            )
            return (new_state, inside + from_state)

        inputs = (
            x_step.reshape(n_blocks, BLOCK, chan_width),
            b_mat.reshape(n_blocks, BLOCK, n_state),
            c_mat.reshape(n_blocks, BLOCK, n_state),
            decay_local.reshape(n_blocks, BLOCK, local_heads),
            seg_here.reshape(n_blocks, BLOCK),
            seg_before,
        )
        final_state, block_out = lax.scan(
            jax.checkpoint(block_step), jnp.zeros((n_state, chan_width), jnp.float32), inputs
        )
        skip_channels = jnp.dot(skip_local, select, precision=HIGH)
        mixer_out = block_out.reshape(length, chan_width) + x_conv * skip_channels[None, :]
        part_cum = jnp.cumsum(decay_local, axis=0)
        carried_in = (seg_here == seg_ext[CONV - 2]).astype(jnp.float32)
        enter = jnp.dot(jnp.exp(part_cum) * carried_in[:, None], select, precision=HIGH)
        return (mixer_out, final_state, enter, c_mat)

    return mixer


def on_device(
    hidden,
    cotangent,
    seg_ids,
    norm_gain,
    in_weight,
    conv_weight,
    conv_bias,
    dt_bias,
    a_log,
    d_skip,
    out_gain,
    out_weight,
):
    gains_in, w_in, w_conv, b_conv, gains_out, w_out = (
        lax.all_gather(norm_gain, "shard", axis=0, tiled=True),
        lax.all_gather(in_weight, "shard", axis=0, tiled=True),
        lax.all_gather(conv_weight, "shard", axis=1, tiled=True),
        lax.all_gather(conv_bias, "shard", axis=0, tiled=True),
        lax.all_gather(out_gain, "shard", axis=0, tiled=True),
        lax.all_gather(out_weight, "shard", axis=0, tiled=True),
    )
    seq_count = lax.axis_size("seq")
    shard_count = lax.axis_size("shard")
    seq_rank = lax.axis_index("seq")
    shard_rank = lax.axis_index("shard")
    tok_len = hidden.shape[0]
    inner_width = w_out.shape[0]
    n_state = (w_conv.shape[1] - inner_width) // 2
    chan_width = inner_width // seq_count
    part_len = tok_len * seq_count
    hidden_f = hidden.astype(jnp.float32)
    gains_f = gains_in.astype(jnp.float32)
    normed_in = token_norm(hidden_f, gains_f).astype(jnp.bfloat16)
    projected = jnp.dot(normed_in, w_in, preferred_element_type=jnp.float32).astype(jnp.bfloat16)
    gate_z = projected[:, :inner_width]
    x_tokens = projected[:, inner_width : 2 * inner_width]
    shared_tokens = projected[:, 2 * inner_width :]
    x_heads = lax.all_to_all(x_tokens, "seq", split_axis=1, concat_axis=0, tiled=True)
    shared = lax.all_gather(shared_tokens, "seq", axis=0, tiled=True)
    bc_heads = shared[:, : 2 * n_state]
    tail_x, tail_bc = from_behind(
        (x_heads[part_len - CONV + 1 :], bc_heads[part_len - CONV + 1 :]), "shard", 1
    )
    lead = jnp.full((CONV - 1,), -1, jnp.int32)
    seg_all = jnp.concatenate([lead, seg_ids])
    seg_ext = lax.dynamic_slice_in_dim(seg_all, shard_rank * part_len, part_len + CONV - 1)
    channel_lo = seq_rank * chan_width
    head_lo = channel_lo // HEAD_DIM
    conv_f = w_conv.astype(jnp.float32)
    bias_f = b_conv.astype(jnp.float32)
    primals = (
        x_heads.astype(jnp.float32),
        bc_heads.astype(jnp.float32),
        shared[:, 2 * n_state :].astype(jnp.float32),
        tail_x.astype(jnp.float32),
        tail_bc.astype(jnp.float32),
        lax.dynamic_slice_in_dim(conv_f, channel_lo, chan_width, 1),
        lax.dynamic_slice_in_dim(bias_f, channel_lo, chan_width, 0),
        conv_f[:, inner_width:],
        bias_f[inner_width:],
        dt_bias.astype(jnp.float32),
        a_log.astype(jnp.float32),
        d_skip.astype(jnp.float32),
    )
    mixer = make_mixer(seg_ext, head_lo, channel_lo)
    mixer_outs, mixer_pull = jax.vjp(mixer, *primals)
    local_out, state_local, enter, c_mat = mixer_outs
    identity = (jnp.ones((chan_width,), jnp.float32), jnp.zeros((n_state, chan_width), jnp.float32))
    state_in = prefix((enter[part_len - 1], state_local), "shard", chain_pairs, identity, False)[1]
    carried = jnp.dot(c_mat, state_in, precision=HIGH)
    mixer_full = local_out + carried * enter
    mixer_tokens = lax.all_to_all(
        mixer_full.astype(jnp.bfloat16), "seq", split_axis=0, concat_axis=1, tiled=True
    )
    normed_f, gate_pull = jax.vjp(
        gate_norm,
        mixer_tokens.astype(jnp.float32),
        gate_z.astype(jnp.float32),
        gains_out.astype(jnp.float32),
    )
    normed_out = normed_f.astype(jnp.bfloat16)
    branch = jnp.dot(normed_out, w_out, preferred_element_type=jnp.float32)
    block_out = (hidden_f + branch).astype(jnp.bfloat16)
    grad_out_w = lax.dot_general(
        normed_out, cotangent, (((0,), (0,)), ((), ())), preferred_element_type=jnp.float32
    )
    d_normed = lax.dot_general(
        cotangent, w_out, (((1,), (1,)), ((), ())), preferred_element_type=jnp.float32
    )
    d_mixer, d_gate_z, d_gain_out = gate_pull(d_normed)
    d_heads = lax.all_to_all(
        d_mixer.astype(jnp.bfloat16), "seq", split_axis=1, concat_axis=0, tiled=True
    ).astype(jnp.float32)
    weighted = d_heads * enter
    d_state_local = jnp.dot(c_mat.T, weighted, precision=HIGH)
    d_state_out = prefix(
        (enter[part_len - 1], d_state_local), "shard", chain_pairs, identity, True
    )[1]
    d_enter = d_heads * carried
    d_enter = d_enter.at[part_len - 1].add(jnp.sum(d_state_out * state_in, axis=0))
    d_c_mat = jnp.dot(weighted, state_in.T, precision=HIGH)
    mixer_grads = mixer_pull((d_heads, d_state_out, d_enter, d_c_mat))
    (
        d_x_raw,
        d_bc_raw,
        d_dt_raw,
        d_tail_x,
        d_tail_bc,
        d_conv_x,
        d_bias_x,
        d_conv_bc,
        d_bias_bc,
        d_dt_bias,
        d_a_log,
        d_d_skip,
    ) = mixer_grads
    back_x, back_bc = from_behind((d_tail_x, d_tail_bc), "shard", -1)
    d_x_raw = d_x_raw.at[part_len - CONV + 1 :].add(back_x)
    d_bc_raw = d_bc_raw.at[part_len - CONV + 1 :].add(back_bc)
    d_x_tokens = lax.all_to_all(
        d_x_raw.astype(jnp.bfloat16), "seq", split_axis=0, concat_axis=1, tiled=True
    )
    d_shared = lax.psum_scatter(
        jnp.concatenate([d_bc_raw, d_dt_raw], 1).astype(jnp.bfloat16),
        "seq",
        scatter_dimension=0,
        tiled=True,
    ).astype(jnp.float32)
    d_projected = jnp.concatenate([d_gate_z, d_x_tokens.astype(jnp.float32), d_shared], 1).astype(
        jnp.bfloat16
    )
    grad_in_w = lax.dot_general(
        normed_in, d_projected, (((0,), (0,)), ((), ())), preferred_element_type=jnp.float32
    )
    d_normed_in = lax.dot_general(
        d_projected, w_in, (((1,), (1,)), ((), ())), preferred_element_type=jnp.float32
    )
    _, norm_pull = jax.vjp(token_norm, hidden_f, gains_f)
    d_hidden_norm, d_gain_in = norm_pull(d_normed_in)
    grad_hidden = cotangent.astype(jnp.float32) + d_hidden_norm
    conv_grad = jnp.zeros(w_conv.shape, jnp.float32)
    conv_grad = lax.dynamic_update_slice(conv_grad, d_conv_x, (jnp.int32(0), channel_lo))
    conv_grad = conv_grad.at[:, inner_width:].set(d_conv_bc)
    bias_grad = jnp.zeros(b_conv.shape, jnp.float32)
    bias_grad = lax.dynamic_update_slice(bias_grad, d_bias_x, (channel_lo,))
    bias_grad = bias_grad.at[inner_width:].set(d_bias_bc)
    head_grads = jnp.concatenate([d_dt_bias, d_a_log, d_d_skip])
    n_heads = dt_bias.shape[0]
    head_rows = jnp.broadcast_to(
        head_grads[None, :], (shard_count * seq_count, head_grads.shape[0])
    )
    partial_sums = (
        lax.psum_scatter(
            d_gain_in.astype(jnp.bfloat16), "shard", scatter_dimension=0, tiled=True
        ).astype(jnp.float32),
        lax.psum_scatter(
            grad_in_w.astype(jnp.bfloat16), "shard", scatter_dimension=0, tiled=True
        ).astype(jnp.float32),
        lax.psum_scatter(
            conv_grad.astype(jnp.bfloat16), "shard", scatter_dimension=1, tiled=True
        ).astype(jnp.float32),
        lax.psum_scatter(
            bias_grad.astype(jnp.bfloat16), "shard", scatter_dimension=0, tiled=True
        ).astype(jnp.float32),
        lax.psum_scatter(
            d_gain_out.astype(jnp.bfloat16), "shard", scatter_dimension=0, tiled=True
        ).astype(jnp.float32),
        lax.psum_scatter(
            grad_out_w.astype(jnp.bfloat16), "shard", scatter_dimension=0, tiled=True
        ).astype(jnp.float32),
        lax.psum_scatter(
            head_rows.astype(jnp.bfloat16), "shard", scatter_dimension=0, tiled=True
        ).astype(jnp.float32),
    )
    reduced = (
        lax.psum_scatter(
            partial_sums[0].astype(jnp.bfloat16), "seq", scatter_dimension=0, tiled=True
        ).astype(jnp.float32),
        lax.psum_scatter(
            partial_sums[1].astype(jnp.bfloat16), "seq", scatter_dimension=0, tiled=True
        ).astype(jnp.float32),
        lax.psum_scatter(
            partial_sums[2].astype(jnp.bfloat16), "seq", scatter_dimension=1, tiled=True
        ).astype(jnp.float32),
        lax.psum_scatter(
            partial_sums[3].astype(jnp.bfloat16), "seq", scatter_dimension=0, tiled=True
        ).astype(jnp.float32),
        lax.psum_scatter(
            partial_sums[4].astype(jnp.bfloat16), "seq", scatter_dimension=0, tiled=True
        ).astype(jnp.float32),
        lax.psum_scatter(
            partial_sums[5].astype(jnp.bfloat16), "seq", scatter_dimension=0, tiled=True
        ).astype(jnp.float32),
        lax.psum_scatter(
            partial_sums[6].astype(jnp.bfloat16), "seq", scatter_dimension=0, tiled=True
        ).astype(jnp.float32),
    )
    head_total = reduced[6][0]
    return (
        block_out,
        grad_hidden,
        reduced[0],
        reduced[1],
        reduced[2],
        reduced[3],
        head_total[:n_heads],
        head_total[n_heads : 2 * n_heads],
        head_total[2 * n_heads :],
        reduced[4],
        reduced[5],
    )


def solution(mesh):
    return jax.shard_map(
        on_device,
        mesh=mesh,
        in_specs=(
            P(("shard", "seq"), None),
            P(("shard", "seq"), None),
            P(),
            P("shard"),
            P("shard", None),
            P(None, "shard"),
            P("shard"),
            P(),
            P(),
            P(),
            P("shard"),
            P("shard", None),
        ),
        out_specs=(
            P(("shard", "seq"), None),
            P(("shard", "seq"), None),
            P(("shard", "seq")),
            P(("shard", "seq"), None),
            P(None, ("shard", "seq")),
            P(("shard", "seq")),
            P(),
            P(),
            P(),
            P(("shard", "seq")),
            P(("shard", "seq"), None),
        ),
        check_vma=False,
    )
```

profile of v0, /device:TPU:0, one launch (start us, length us, event | category | flops | bytes accessed | tf_op | source)
XLA Modules:
  0.0 2106.3 jit_solution(14078692126944660812)
XLA Ops:
  8.0 6.1 all-gather.2
  15.2 122.0 %all-gather.10.cloned.1.call-done = bf16[1536,6448]{0,1:T(8,128)(2,1)} async-done(((bf16[384,6448]{0,1:T(8,128)(2,1)}), bf16[1536,6448]{0,1:T(8,128)(2,1)}) %all-gather.10.cloned.1.call-update) | async-done | bytes 19808272 | tf_op jit(solution)/shard_map/all_gather | solution.py:180
  137.2 15.2 convolution_convert_fusion.2
  159.5 5.2 all-gather.3
  166.3 6.5 all-reduce.24
  179.9 5.3 all-to-all-start
  185.2 47.3 %all-gather.12.cloned.1.call-done = bf16[4096,304]{0,1:T(8,128)(2,1)} async-done(((bf16[512,304]{0,1:T(8,128)(2,1)}), bf16[4096,304]{0,1:T(8,128)(2,1)}) %all-gather.12.cloned.1.call-update) | async-done | bytes 2490384 | tf_op jit(solution)/shard_map/all_gather | solution.py:203
  250.2 5.2 all-gather.4
  256.3 5.0 fusion.151
  270.5 4.9 all-to-all-done
  286.1 19.9 fusion.198
  309.5 309.7 %while.75 = (s32[]{:T(128)}, f32[128,384]{1,0:T(8,128)S(1)}, f32[16,256,384]{2,1,0:T(8,128)}, f32[16,128,384]{2,1,0:T(8,128)}, f32[16,256,7]{1,2,0:T(8,128)}, /*...) while((s32[]{:T(128)}, f32[128,384]{1,0:T(8,128)S(1)}, ...), condition=%wide.region_5.6_spmd.clone.clone.clone, body=%wide.region_1.5_spmd.clone.clone.clone.sunk | while | flops 2536740608 | bytes 5860804 | solution.py:151
  619.2 6.9 all-gather
  626.6 12.8 fusion.144
  642.3 12.3 all-to-all-start.1
  654.6 5.2 all-gather.5
  659.8 66.1 %all-to-all-done.1 = bf16[8,512,384]{1,2,0:T(8,128)(2,1)S(1)} async-done(((bf16[8,512,384]{1,2,0:T(8,128)(2,1)}), bf16[8,512,384]{1,2,0:T(8,128)(2,1)S(1)}, u32[]{:S(2)}, u32[]{:S(2)}) %all-to-all-start.1) | async-done | bytes 3145760 | tf_op jit(solution)/shard_map/all_to_all | solution.py:236
  725.9 5.3 multiply_reduce_fusion.9
  731.9 12.6 multiply_reduce_fusion.3
  744.6 7.7 fusion.138
  756.1 70.7 %all-to-all-done.2 = bf16[512,8,384]{0,2,1:T(8,128)(2,1)S(1)} async-done(((bf16[512,8,384]{0,2,1:T(8,128)(2,1)}), bf16[512,8,384]{0,2,1:T(8,128)(2,1)S(1)}, u32[]{:S(2)}, u32[]{:S(2)}) %all-to-all-start.2) | async-done | bytes 3145760 | tf_op jit(solution)/shard_map/all_to_all | solution.py:255
  830.3 6.6 copy.137
  836.9 5.4 bitcast_multiply_fusion.4
  847.0 6.1 all-gather.1
  860.6 557.6 %while.74 = (s32[]{:T(128)}, f32[128,384]{1,0:T(8,128)S(1)}, f32[16,256,384]{2,1,0:T(8,128)}, f32[16,256,128]{2,1,0:T(8,128)}, f32[16,256,128]{2,1,0:T(8,128)}, ...) while((s32[]{:T(128)}, f32[128,384]{1,0:T(8,128)S(1)}, ...), condition=%wide.region_24.25_spmd.clone, body=%wide.region_14.24_spmd.clone.sunk | while | flops 5326403584 | bytes 15732097 | solution.py:151
  886.5 8.8 reduce-window.100
  921.3 8.8 reduce-window.100
  956.0 8.8 reduce-window.100
  990.8 8.8 reduce-window.100
  1025.6 8.8 reduce-window.100
  1060.4 8.8 reduce-window.100
  1095.2 8.8 reduce-window.100
  1130.0 8.8 reduce-window.100
  1164.8 8.8 reduce-window.100
  1199.7 8.8 reduce-window.100
  1234.5 8.8 reduce-window.100
  1269.3 8.8 reduce-window.100
  1304.2 8.8 reduce-window.100
  1339.0 8.8 reduce-window.100
  1373.8 8.8 reduce-window.100
  1408.6 8.8 reduce-window.100
  1424.2 10.2 convolution_add_fusion.4
  1434.5 6.2 multiply_reduce_fusion.12
  1440.7 5.1 broadcast_multiply_fusion.1
  1445.8 11.0 pad_add_fusion.1
  1458.8 23.2 %multiply_reduce_fusion.6 = (f32[384]{0:T(512)}, f32[384]{0:T(512)}, f32[384]{0:T(512)}, bf16[384]{0:T(512)(128)(2,1)}, f32[384]{0:T(512)}, /*index=5*/f32[4096,...) fusion(f32[4096,384]{1,0:T(8,128)} %bitcast_convert_fusion, ...), kind=kLoop, calls=%fused_computation.197 | loop fusion | flops 51902208 | bytes 59832576 | tf_op jit(solution)/shard_map/transpose(jvp())/reduce_sum | solution.py:62
  1486.1 5.7 fusion.161
  1491.8 8.7 reduce-window.80
  1501.1 5.8 fusion.175
  1521.1 10.4 convolution_convert_fusion.1
  1532.2 5.8 broadcast_multiply_fusion
  1548.5 4.7 copy.141
  1557.8 83.6 %reduce-scatter.15.cloned.1.call-done = bf16[512,304]{0,1:T(8,128)(2,1)} async-done(((bf16[4096,304]{0,1:T(8,128)(2,1)}), bf16[512,304]{0,1:T(8,128)(2,1)}) %reduce-scatter.15.cloned.1.call-update) | async-done | bytes 311312 | tf_op jit(solution)/shard_map/reduce_scatter | solution.py:287
  1641.4 17.4 convolution_convert_fusion
  1658.9 25.0 %copy.152 = bf16[1536,6448]{1,0:T(8,128)(2,1)} copy(bf16[1536,6448]{0,1:T(8,128)(2,1)} %convolution_convert_fusion) | data formatting | bytes 39616512
  1687.2 33.3 %reduce-scatter.19.cloned.1.call-done = bf16[768,1536]{1,0:T(8,128)(2,1)} async-done(((bf16[3072,1536]{1,0:T(8,128)(2,1)}), bf16[768,1536]{1,0:T(8,128)(2,1)}) %reduce-scatter.19.cloned.1.call-update) | async-done | bytes 2359312 | tf_op jit(solution)/shard_map/reduce_scatter | solution.py:332
  1720.5 149.7 %reduce-scatter.23.cloned.1.call-done = bf16[384,6448]{1,0:T(8,128)(2,1)} async-done(((bf16[1536,6448]{1,0:T(8,128)(2,1)}), bf16[384,6448]{1,0:T(8,128)(2,1)}) %reduce-scatter.23.cloned.1.call-update) | async-done | bytes 4952080
  1874.8 11.1 fusion.159
  1886.2 10.9 reduce-scatter.27.cloned.1.call-done
  1898.2 20.3 fusion.155
  1918.4 10.2 all-reduce.34
  1928.9 37.7 %all-reduce.33 = (bf16[384]{0:T(512)(128)(2,1)S(1)}, bf16[4,832]{1,0:T(4,128)(2,1)S(1)}, bf16[832]{0:T(1024)(128)(2,1)S(1)}, bf16[8,144]{1,0:T(8,128)(2,1)S(1)}, bf16[768]{0:T(1024)(128)(2,1)S(1)}) all-reduce(bf16[384]{0:T(512)(128)(2,1)S(1)} %dynamic-slice.41, ...), channel_id=6, replica_groups=mesh['shard'=4,'seq'=8] {'seq'}, use_global_device_ids=true, to_apply=%region_32.33.clone | all-reduce | flops 6464 | bytes 25856
  1974.7 17.7 reduce-scatter.21.cloned.1.call-done
  1994.2 100.6 %reduce-scatter.25.cloned.1.call-done = bf16[48,6448]{1,0:T(8,128)(2,1)} async-done(((bf16[384,6448]{1,0:T(8,128)(2,1)}), bf16[48,6448]{1,0:T(8,128)(2,1)}) %reduce-scatter.25.cloned.1.call-update) | async-done | bytes 619024
  (1492 shorter events, 866.8 us)
Async XLA Ops:
  7.2 130.0 %all-gather.10.cloned.1.call-start = ((), (), s32[]{:S(2)}) async-start(), calls=%async_computation.11 | async-start | bytes 24760320 | tf_op jit(solution)/shard_map/all_gather | solution.py:180
  7.9 224.5 %all-gather.12.cloned.1.call-start = ((), (), s32[]{:S(2)}) async-start(), calls=%async_computation.12 | async-start | bytes 2801664 | tf_op jit(solution)/shard_map/all_gather | solution.py:203
  14.1 138.3 %copy-start.32 = (f32[1536]{0:T(1024)}, f32[1536]{0:T(1024)S(1)}, u32[]{:S(2)}) copy-start(f32[1536]{0:T(1024)S(1)} %reshape.690) | copy-start | bytes 18436
  15.1 137.3 %copy-start.56 = (f32[512]{0:T(512)}, f32[512]{0:T(512)S(1)}, u32[]{:S(2)}) copy-start(f32[512]{0:T(512)S(1)} %fusion.186) | copy-start | bytes 6148
  15.1 141.6 %copy-start.85 = (bf16[48]{0:T(256)(128)(2,1)S(1)}, bf16[48]{0:T(256)(128)(2,1)}, u32[]{:S(2)}) copy-start(bf16[48]{0:T(256)(128)(2,1)} %param.37) | copy-start | bytes 292
  15.1 141.6 %copy-start.87 = (bf16[48]{0:T(256)(128)(2,1)S(1)}, bf16[48]{0:T(256)(128)(2,1)}, u32[]{:S(2)}) copy-start(bf16[48]{0:T(256)(128)(2,1)} %param.38) | copy-start | bytes 292
  15.2 141.6 %copy-start.27 = (s32[16384]{0:T(1024)S(1)}, s32[16384]{0:T(1024)}, u32[]{:S(2)}) copy-start(s32[16384]{0:T(1024)} %param.32) | copy-start | bytes 196612
  15.2 144.3 %copy-start.61 = (bf16[4,832]{1,0:T(4,128)(2,1)S(1)}, bf16[4,832]{1,0:T(4,128)(2,1)}, u32[]{:S(2)}) copy-start(bf16[4,832]{1,0:T(4,128)(2,1)} %param.35) | copy-start | bytes 19972
  15.2 149.6 %copy-start.71 = (u32[32]{0:T(128)S(1)}, u32[32]{0:T(128)}, u32[]{:S(2)}) copy-start(u32[32]{0:T(128)} %constant.423) | copy-start | bytes 388
  15.2 150.9 %copy-start.72 = (bf16[832]{0:T(1024)(128)(2,1)S(1)}, bf16[832]{0:T(1024)(128)(2,1)}, u32[]{:S(2)}) copy-start(bf16[832]{0:T(1024)(128)(2,1)} %param.36) | copy-start | bytes 4996
  15.2 160.0 %copy-start.86 = (bf16[48]{0:T(256)(128)(2,1)S(1)}, bf16[48]{0:T(256)(128)(2,1)}, u32[]{:S(2)}) copy-start(bf16[48]{0:T(256)(128)(2,1)} %param.39) | copy-start | bytes 292
  155.9 576.0 %all-gather.14.cloned.1.call-start = ((), (), s32[]{:S(2)}) async-start(), calls=%async_computation.13 | async-start | bytes 11796480 | tf_op jit(solution)/shard_map/all_gather | solution.py:184
  156.7 80.1 %copy-start.75 = (f32[48]{0:T(128)}, f32[48]{0:T(128)S(1)}, u32[]{:S(2)}) copy-start(f32[48]{0:T(128)S(1)} %convert_element_type.243) | copy-start | bytes 580
  156.8 80.0 %copy-start.77 = (f32[48]{0:T(128)}, f32[48]{0:T(128)S(1)}, u32[]{:S(2)}) copy-start(f32[48]{0:T(128)S(1)} %convert_exponential_fusion) | copy-start | bytes 580
  158.1 87.2 %copy-start.30 = (f32[4096]{0:T(1024)}, f32[4096]{0:T(1024)S(1)}, u32[]{:S(2)}) copy-start(f32[4096]{0:T(1024)S(1)} %get-tuple-element.1069) | copy-start | bytes 49156
  174.6 81.7 %copy-start.36 = (f32[1,256]{1,0:T(1,128)}, f32[1,256]{1,0:T(1,128)S(1)}, u32[]{:S(2)}) copy-start(f32[1,256]{1,0:T(1,128)S(1)} %get-tuple-element.1109) | copy-start | bytes 3076
  174.6 81.7 %copy-start.38 = (f32[1,256]{1,0:T(1,128)}, f32[1,256]{1,0:T(1,128)S(1)}, u32[]{:S(2)}) copy-start(f32[1,256]{1,0:T(1,128)S(1)} %get-tuple-element.1110) | copy-start | bytes 3076
  174.6 81.7 %copy-start.40 = (f32[1,256]{1,0:T(1,128)}, f32[1,256]{1,0:T(1,128)S(1)}, u32[]{:S(2)}) copy-start(f32[1,256]{1,0:T(1,128)S(1)} %get-tuple-element.1111) | copy-start | bytes 3076
  179.9 95.5 %all-to-all-start = ((bf16[512,8,384]{0,2,1:T(8,128)(2,1)}), bf16[512,8,384]{0,2,1:T(8,128)(2,1)S(1)}, u32[]{:S(2)}, u32[]{:S(2)}) async-start(bf16[512,8,384]{0,2,1:T(8,128)(2,1)} %bitcast.462), calls=%async_computation | async-start | bytes 6291456 | tf_op jit(solution)/shard_map/all_to_all | solution.py:202
  234.0 21.4 %collective-permute-start = (bf16[3,256]{0,1:T(8,128)(2,1)}, bf16[3,256]{0,1:T(8,128)(2,1)}, u32[]{:S(2)}, u32[]{:S(2)}) collective-permute-start(bf16[3,256]{0,1:T(8,128)(2,1)} %slice.392), channel_id=1, source_target_pairs={{0,8},{8,16},{16,24},{1,9},{9,17},{17,25},{2,10},{10,18},{18,26},{... | collective-permute-start | bytes 4616 | tf_op jit(solution)/shard_map/ppermute | solution.py:16
  248.9 7.4 copy-start.42
  248.9 7.4 copy-start.64
  250.2 11.1 copy-start.3
  280.7 5.3 collective-permute-start.1
  309.5 317.1 %copy-start.69 = (f32[384]{0:T(512)S(1)}, f32[384]{0:T(512)}, u32[]{:S(2)}) copy-start(f32[384]{0:T(512)} %convolution_reduce_fusion) | copy-start | bytes 4612
  642.3 12.3 copy-start.73
  642.3 83.7 %all-to-all-start.1 = ((bf16[8,512,384]{1,2,0:T(8,128)(2,1)}), bf16[8,512,384]{1,2,0:T(8,128)(2,1)S(1)}, u32[]{:S(2)}, u32[]{:S(2)}) async-start(bf16[8,512,384]{1,2,0:T(8,128)(2,1)} %copy.135), calls=%async_computation.1 | async-start | bytes 6291456 | tf_op jit(solution)/shard_map/all_to_all | solution.py:236
  731.9 12.7 slice-start.2
  731.9 12.7 slice-start.3
  731.9 12.7 copy-start.59
  752.2 74.6 %all-to-all-start.2 = ((bf16[512,8,384]{0,2,1:T(8,128)(2,1)}), bf16[512,8,384]{0,2,1:T(8,128)(2,1)S(1)}, u32[]{:S(2)}, u32[]{:S(2)}) async-start(bf16[512,8,384]{0,2,1:T(8,128)(2,1)} %bitcast.464), calls=%async_computation.2 | async-start | bytes 6291456 | tf_op jit(solution)/shard_map/all_to_all | solution.py:255
  755.9 885.5 %reduce-scatter.15.cloned.1.call-start = ((), (), s32[]{:S(2)}) async-start(), calls=%async_computation.14 | async-start | bytes 2801664 | tf_op jit(solution)/shard_map/reduce_scatter | solution.py:287
  1421.1 13.3 copy-start.15
  1424.2 10.2 copy-start.4
  1424.2 10.2 copy-start.11
  1424.2 10.2 copy-start.18
  1445.8 11.0 copy-start
  1445.8 13.0 slice-start
  1445.8 13.0 slice-start.1
  1458.8 25.9 %copy-start.58 = (f32[384]{0:T(512)S(1)}, f32[384]{0:T(512)}, u32[]{:S(2)}) copy-start(f32[384]{0:T(512)} %multiply_reduce_fusion.15) | copy-start | bytes 4612
  1458.8 27.3 %copy-start.25 = (f32[1,7,32,128]{3,2,1,0:T(8,128)S(1)}, f32[1,7,32,128]{3,2,1,0:T(8,128)}, u32[]{:S(2)}) copy-start(f32[1,7,32,128]{3,2,1,0:T(8,128)} %copy-done.24) | copy-start | bytes 344068
  1458.8 27.3 %copy-start.31 = (f32[4096]{0:T(1024)S(1)}, f32[4096]{0:T(1024)}, u32[]{:S(2)}) copy-start(f32[4096]{0:T(1024)} %copy-done.30) | copy-start | bytes 49156
  1491.8 16.4 copy-start.29
  1501.1 11.0 copy-start.76
  1501.1 11.0 copy-start.78
  1501.1 13.9 copy-start.16
  1506.9 10.3 collective-permute-start.3
  1521.1 199.4 %reduce-scatter.19.cloned.1.call-start = ((), (), s32[]{:S(2)}) async-start(), calls=%async_computation.16 | async-start | bytes 11796480 | tf_op jit(solution)/shard_map/reduce_scatter | solution.py:332
  1538.0 9.2 collective-permute-start.2
  1553.2 88.3 %copy-start.22 = (bf16[512,1536]{1,0:T(8,128)(2,1)S(1)}, bf16[512,1536]{1,0:T(8,128)(2,1)}, u32[]{:S(2)}) copy-start(bf16[512,1536]{1,0:T(8,128)(2,1)} %param.30) | copy-start | bytes 4718596
  1553.2 88.3 %copy-start.33 = (f32[1536]{0:T(1024)S(1)}, f32[1536]{0:T(1024)}, u32[]{:S(2)}) copy-start(f32[1536]{0:T(1024)} %copy-done.32) | copy-start | bytes 18436
  1553.2 88.3 %copy-start.57 = (f32[512]{0:T(512)S(1)}, f32[512]{0:T(512)}, u32[]{:S(2)}) copy-start(f32[512]{0:T(512)} %copy-done.56) | copy-start | bytes 6148
  1553.2 88.3 %all-to-all-start.3 = ((bf16[8,512,384]{1,2,0:T(8,128)(2,1)}), bf16[8,512,384]{1,2,0:T(8,128)(2,1)}, u32[]{:S(2)}, u32[]{:S(2)}) async-start(bf16[8,512,384]{1,2,0:T(8,128)(2,1)} %copy.141), calls=%async_computation.3 | async-start | bytes 6291456 | tf_op jit(solution)/shard_map/all_to_all | solution.py:284
  1557.8 312.5 %reduce-scatter.23.cloned.1.call-start = ((), (), s32[]{:S(2)}) async-start(), calls=%async_computation.18 | async-start | bytes 25067520
  1684.0 213.1 %reduce-scatter.27.cloned.1.call-start = ((), (), s32[]{:S(2)}) async-start(), calls=%async_computation.20 | async-start | bytes 1064960
  1685.9 186.3 %copy-start.89 = (u32[32]{0:T(128)S(1)}, u32[32]{0:T(128)}, u32[]{:S(2)}) copy-start(u32[32]{0:T(128)} %constant.433) | copy-start | bytes 388
  1686.1 242.8 %reduce-scatter.17.cloned.1.call-start = ((), (), s32[]{:S(2)}) async-start(), calls=%async_computation.15 | async-start | bytes 20480 | tf_op jit(solution)/shard_map/reduce_scatter | solution.py:335
  1687.1 305.3 %reduce-scatter.21.cloned.1.call-start = ((), (), s32[]{:S(2)}) async-start(), calls=%async_computation.17 | async-start | bytes 2654208 | tf_op jit(solution)/shard_map/reduce_scatter | solution.py:355
  1720.5 374.4 %reduce-scatter.25.cloned.1.call-start = ((), (), s32[]{:S(2)}) async-start(), calls=%async_computation.19 | async-start | bytes 5640192
  1874.8 11.2 copy-start.63
  1874.8 11.4 copy-start.81
  1898.2 20.3 copy-start.62
  1898.2 72.1 %copy-start.35 = (f32[512]{0:T(512)S(1)}, f32[512]{0:T(512)}, u32[]{:S(2)}) copy-start(f32[512]{0:T(512)} %copy-done.34) | copy-start | bytes 6148
  1898.2 72.1 %copy-start.23 = (bf16[512,1536]{1,0:T(8,128)(2,1)S(1)}, bf16[512,1536]{1,0:T(8,128)(2,1)}, u32[]{:S(2)}) copy-start(bf16[512,1536]{1,0:T(8,128)(2,1)} %param.31) | copy-start | bytes 4718596
  (48 other events, 153.2 us)
Sparse Core Ops, SparseCore 0:
  9.6 127.5 all-gather.9
  156.0 76.4 all-gather.11
  234.0 75.5 all-gather.13
  1521.2 120.1 reduce-scatter.14
  1644.0 76.3 reduce-scatter.18
  1723.1 147.1 reduce-scatter.22
  1873.4 23.6 reduce-scatter.26
  1900.2 19.3 reduce-scatter.16
  1923.1 69.2 reduce-scatter.20
  1995.9 98.9 reduce-scatter.24
where the time goes:
time: 2120 us; the launch traced here: 2110 us
  waiting for transfers between devices  708 us (33%)
  matrix products  579 us (27%)
  other arithmetic  393 us (19%)
  local copies, waits for them, and re-layouts  278 us (13%)
  blocking collectives  89 us (4%)
  starting transfers between devices  33.7 us (2%)
    unnamed x13, waiting for transfers between devices  263 us
    another operation x102, other arithmetic  231 us
    dot_general x48, matrix products, block_step(): jnp.einsum('jts,sc->jtc', weights * scores[None], x_block, precision=HIGH)  198 us
    all_gather x1, waiting for transfers between devices, on_device(): lax.all_gather(in_weight, 'shard', axis=0, tiled=True)  122 us
    reduce_scatter x1, waiting for transfers between devices, on_device(): lax.psum_scatter(jnp.concatenate([d_bc_raw, d_dt_raw], 1).astype(jnp.bflo...  83.6 us
    all_to_all x1, waiting for transfers between devices, on_device(): lax.all_to_all(d_mixer.astype(jnp.bfloat16), 'seq', split_axis=1, concat_...  70.7 us
    all_to_all x1, waiting for transfers between devices, on_device(): lax.all_to_all(mixer_full.astype(jnp.bfloat16), 'seq', split_axis=0, conc...  66.1 us
    dot_general x64, matrix products, block_step(): scores = jnp.dot(c_block, b_block.T, precision=HIGH)  64.3 us
  transfers between devices with their start and end apart: 18, of which 11 were waited for; matrix products, arithmetic and copies ran while one was open for 25% of the time, Pallas kernels for 0%

commit v1 on v0

--- a/solution.py
+++ b/solution.py
@@ -175,9 +175,24 @@
     out_gain,
     out_weight,
 ):
+
+    def find_things(page, lane_axis, which_dim):
+        vec_out = lax.axis_size(lane_axis)
+        h_now = lax.axis_index(lane_axis)
+        opened, d_next, built = (vec_out, h_now, page.shape[which_dim])
+        new, step_out = (page, 1)
+        while step_out < opened:
+            w2 = range(opened)
+            outer = map(lambda pp: (pp, (pp - step_out) % opened), w2)
+            field_out = list(outer)
+            e_now = lax.ppermute(new, axis_name=lane_axis, perm=field_out)
+            new = jnp.concatenate([new, e_now], axis=which_dim)
+            step_out = 2 * step_out
+        return jnp.roll(new, d_next * built, axis=which_dim)
+
     gains_in, w_in, w_conv, b_conv, gains_out, w_out = (
         lax.all_gather(norm_gain, "shard", axis=0, tiled=True),
-        lax.all_gather(in_weight, "shard", axis=0, tiled=True),
+        find_things(in_weight, "shard", 0),
         lax.all_gather(conv_weight, "shard", axis=1, tiled=True),
         lax.all_gather(conv_bias, "shard", axis=0, tiled=True),
         lax.all_gather(out_gain, "shard", axis=0, tiled=True),

time: 2120 us -> 2310 us (1.090)
  blocking collectives: 89 us -> 300 us
  waiting for transfers between devices: 708 us -> 637 us
  local copies, waits for them, and re-layouts: 278 us -> 312 us
    all_gather x1, blocking collectives: 6.09 us -> 216 us  [on_device(): lax.all_gather(norm_gain, 'shard', axis=0, tiled=True)]
    all_gather x1 -> x0, waiting for transfers between devices: 122 us -> none  [on_device(): lax.all_gather(in_weight, 'shard', axis=0, tiled=True)]
    ppermute x0 -> x2, waiting for transfers between devices: none -> 54.5 us  [find_things(): e_now = lax.ppermute(new, axis_name=lane_axis, perm=field_out)]
    unnamed x209 -> x216, local copies, waits for them, and re-layouts: 51.5 us -> 76.9 us
    unnamed x13 -> x12, waiting for transfers between devices: 263 us -> 262 us
  transfers between devices with their start and end apart: 18 -> 19, of which waited for: 11 -> 11; matrix products, arithmetic and copies ran while one was open for 25% -> 23% of each run, Pallas kernels for 0% -> 0%
where the time goes in v1:
time: 2310 us; the launch traced here: 2300 us
  waiting for transfers between devices  637 us (28%)
  matrix products  582 us (25%)
  other arithmetic  404 us (17%)
  local copies, waits for them, and re-layouts  312 us (14%)
  blocking collectives  300 us (13%)
  starting transfers between devices  37.3 us (2%)
    unnamed x12, waiting for transfers between devices  262 us
    another operation x102, other arithmetic  232 us
    all_gather x1, blocking collectives, on_device(): lax.all_gather(norm_gain, 'shard', axis=0, tiled=True)  216 us
    dot_general x48, matrix products, block_step(): jnp.einsum('jts,sc->jtc', weights * scores[None], x_block, precision=HIGH)  198 us
    reduce_scatter x1, waiting for transfers between devices, on_device(): lax.psum_scatter(jnp.concatenate([d_bc_raw, d_dt_raw], 1).astype(jnp.bflo...  83.6 us
    unnamed x216, local copies, waits for them, and re-layouts  76.9 us
    all_to_all x1, waiting for transfers between devices, on_device(): lax.all_to_all(d_mixer.astype(jnp.bfloat16), 'seq', split_axis=1, concat_...  70.4 us
    all_to_all x1, waiting for transfers between devices, on_device(): lax.all_to_all(mixer_full.astype(jnp.bfloat16), 'seq', split_axis=0, conc...  66.1 us
  transfers between devices with their start and end apart: 19, of which 11 were waited for; matrix products, arithmetic and copies ran while one was open for 23% of the time, Pallas kernels for 0%

profile of v1, /device:TPU:0, one launch (start us, length us, event | category | flops | bytes accessed | tf_op | source)
XLA Modules:
  0.0 2296.5 jit_solution(7349704793918331494)
XLA Ops:
  9.7 54.5 %collective-permute-done = bf16[384,6448]{0,1:T(8,128)(2,1)S(1)} collective-permute-done((bf16[384,6448]{0,1:T(8,128)(2,1)}, bf16[384,6448]{0,1:T(8,128)(2,1)S(1)}, u32[]{:S(2)}, u32[]{:S(2)}) %collective-permute-start) | collective-permute-done | bytes 4952096 | tf_op jit(solution)/shard_map/ppermute | solution.py:188
  64.1 7.7 pad_maximum_fusion
  72.4 216.2 %all-gather.2 = bf16[4,1,384]{2,1,0:T(2,128)(2,1)S(1)} all-gather(bf16[1,1,384]{2,1,0:T(2,128)(2,1)S(1)} %reshape.682), channel_id=1, replica_groups=mesh['shard'=4,'seq'=8] {'shard'}, dimensions={0}, use_global_device_ids=true | all-gather | bytes 3840 | tf_op jit(solution)/shard_map/all_gather | solution.py:194
  289.1 5.5 constant_dynamic-update-slice_fusion.5
  297.4 8.3 constant_dynamic-update-slice_fusion.3
  311.0 5.4 constant_dynamic-update-slice_fusion.1
  316.4 8.3 constant_dynamic-update-slice_fusion
  324.8 17.6 fusion.135
  347.7 5.7 all-gather.3
  355.0 6.7 all-reduce.24
  368.7 5.4 all-to-all-start
  374.2 47.1 %all-gather.9.cloned.1.call-done = bf16[4096,304]{0,1:T(8,128)(2,1)} async-done(((bf16[512,304]{0,1:T(8,128)(2,1)}), bf16[4096,304]{0,1:T(8,128)(2,1)}) %all-gather.9.cloned.1.call-update) | async-done | bytes 2490384 | tf_op jit(solution)/shard_map/all_gather | solution.py:218
  474.8 19.7 fusion.206
  497.8 309.6 %while.75 = (s32[]{:T(128)}, f32[128,384]{1,0:T(8,128)S(1)}, f32[16,256,384]{2,1,0:T(8,128)}, f32[16,128,384]{2,1,0:T(8,128)}, f32[16,256,7]{1,2,0:T(8,128)}, /*...) while((s32[]{:T(128)}, f32[128,384]{1,0:T(8,128)S(1)}, ...), condition=%wide.region_5.6_spmd.clone.clone.clone, body=%wide.region_1.5_spmd.clone.clone.clone.sunk | while | flops 2536740608 | bytes 5860804 | solution.py:151
  807.5 6.9 all-gather
  814.6 12.8 fusion.151
  830.3 12.9 all-to-all-start.1
  848.4 66.1 %all-to-all-done.1 = bf16[8,512,384]{1,2,0:T(8,128)(2,1)S(1)} async-done(((bf16[8,512,384]{1,2,0:T(8,128)(2,1)}), bf16[8,512,384]{1,2,0:T(8,128)(2,1)S(1)}, u32[]{:S(2)}, u32[]{:S(2)}) %all-to-all-start.1) | async-done | bytes 3145760 | tf_op jit(solution)/shard_map/all_to_all | solution.py:251
  914.5 5.3 multiply_reduce_fusion.9
  920.4 12.6 multiply_reduce_fusion.3
  933.1 7.8 fusion.145
  944.9 70.4 %all-to-all-done.2 = bf16[512,8,384]{0,2,1:T(8,128)(2,1)S(1)} async-done(((bf16[512,8,384]{0,2,1:T(8,128)(2,1)}), bf16[512,8,384]{0,2,1:T(8,128)(2,1)S(1)}, u32[]{:S(2)}, u32[]{:S(2)}) %all-to-all-start.2) | async-done | bytes 3145760 | tf_op jit(solution)/shard_map/all_to_all | solution.py:270
  1018.9 6.6 copy.137
  1025.6 5.4 bitcast_multiply_fusion.4
  1035.6 6.1 all-gather.1
  1049.2 557.3 %while.74 = (s32[]{:T(128)}, f32[128,384]{1,0:T(8,128)S(1)}, f32[16,256,384]{2,1,0:T(8,128)}, f32[16,256,128]{2,1,0:T(8,128)}, f32[16,256,128]{2,1,0:T(8,128)}, ...) while((s32[]{:T(128)}, f32[128,384]{1,0:T(8,128)S(1)}, ...), condition=%wide.region_24.25_spmd.clone, body=%wide.region_14.24_spmd.clone.sunk | while | flops 5326403584 | bytes 15732097 | solution.py:151
  1075.0 8.8 reduce-window.100
  1109.8 8.8 reduce-window.100
  1144.6 8.8 reduce-window.100
  1179.4 8.8 reduce-window.100
  1214.2 8.8 reduce-window.100
  1249.0 8.8 reduce-window.100
  1283.8 8.8 reduce-window.100
  1318.6 8.8 reduce-window.100
  1353.4 8.8 reduce-window.100
  1388.2 8.8 reduce-window.100
  1423.0 8.8 reduce-window.100
  1457.8 8.8 reduce-window.100
  1492.6 8.8 reduce-window.100
  1527.4 8.8 reduce-window.100
  1562.3 8.8 reduce-window.100
  1597.1 8.8 reduce-window.100
  1612.4 10.2 convolution_add_fusion.4
  1622.7 6.9 multiply_reduce_fusion.12
  1629.6 6.8 broadcast_multiply_fusion.1
  1636.4 11.0 pad_add_fusion.1
  1649.5 23.3 %multiply_reduce_fusion.6 = (f32[384]{0:T(512)}, f32[384]{0:T(512)}, f32[384]{0:T(512)}, bf16[384]{0:T(512)(128)(2,1)}, f32[384]{0:T(512)}, /*index=5*/f32[4096,...) fusion(f32[4096,384]{1,0:T(8,128)} %bitcast_convert_fusion, ...), kind=kLoop, calls=%fused_computation.202 | loop fusion | flops 51902208 | bytes 59832576 | tf_op jit(solution)/shard_map/transpose(jvp())/reduce_sum | solution.py:62
  1676.7 5.7 fusion.167
  1682.4 8.7 reduce-window.80
  1691.7 5.8 fusion.181
  1711.7 10.3 convolution_convert_fusion.1
  1722.7 5.8 broadcast_multiply_fusion
  1748.4 83.6 %reduce-scatter.15.cloned.1.call-done = bf16[512,304]{0,1:T(8,128)(2,1)} async-done(((bf16[4096,304]{0,1:T(8,128)(2,1)}), bf16[512,304]{0,1:T(8,128)(2,1)}) %reduce-scatter.15.cloned.1.call-update) | async-done | bytes 311312 | tf_op jit(solution)/shard_map/reduce_scatter | solution.py:302
  1832.0 17.3 convolution_convert_fusion
  1849.3 25.4 %copy.152 = bf16[1536,6448]{1,0:T(8,128)(2,1)} copy(bf16[1536,6448]{0,1:T(8,128)(2,1)} %convolution_convert_fusion) | data formatting | bytes 39616512
  1878.0 33.0 %reduce-scatter.19.cloned.1.call-done = bf16[768,1536]{1,0:T(8,128)(2,1)} async-done(((bf16[3072,1536]{1,0:T(8,128)(2,1)}), bf16[768,1536]{1,0:T(8,128)(2,1)}) %reduce-scatter.19.cloned.1.call-update) | async-done | bytes 2359312 | tf_op jit(solution)/shard_map/reduce_scatter | solution.py:347
  1911.1 149.7 %reduce-scatter.23.cloned.1.call-done = bf16[384,6448]{1,0:T(8,128)(2,1)} async-done(((bf16[1536,6448]{1,0:T(8,128)(2,1)}), bf16[384,6448]{1,0:T(8,128)(2,1)}) %reduce-scatter.23.cloned.1.call-update) | async-done | bytes 4952080
  2065.3 11.3 fusion.166
  2076.9 10.6 reduce-scatter.27.cloned.1.call-done
  2088.6 21.3 fusion.162
  2109.9 10.2 all-reduce.34
  2120.4 37.8 %all-reduce.33 = (bf16[384]{0:T(512)(128)(2,1)S(1)}, bf16[4,832]{1,0:T(4,128)(2,1)S(1)}, bf16[832]{0:T(1024)(128)(2,1)S(1)}, bf16[8,144]{1,0:T(8,128)(2,1)S(1)}, bf16[768]{0:T(1024)(128)(2,1)S(1)}) all-reduce(bf16[384]{0:T(512)(128)(2,1)S(1)} %dynamic-slice.41, ...), channel_id=6, replica_groups=mesh['shard'=4,'seq'=8] {'seq'}, use_global_device_ids=true, to_apply=%region_32.33.clone | all-reduce | flops 6464 | bytes 25856
  2166.2 16.6 reduce-scatter.21.cloned.1.call-done
  2184.7 100.8 %reduce-scatter.25.cloned.1.call-done = bf16[48,6448]{1,0:T(8,128)(2,1)} async-done(((bf16[384,6448]{1,0:T(8,128)(2,1)}), bf16[48,6448]{1,0:T(8,128)(2,1)}) %reduce-scatter.25.cloned.1.call-update) | async-done | bytes 619024
  (1502 shorter events, 898.9 us)
Async XLA Ops:
  7.2 65.2 %copy-start.81 = (bf16[384]{0:T(512)(128)(2,1)S(1)}, bf16[384]{0:T(512)(128)(2,1)}, u32[]{:S(2)}) copy-start(bf16[384]{0:T(512)(128)(2,1)} %param.33) | copy-start | bytes 2308
  7.2 281.4 %copy-start.22 = (bf16[512,1536]{1,0:T(8,128)(2,1)S(1)}, bf16[512,1536]{1,0:T(8,128)(2,1)}, u32[]{:S(2)}) copy-start(bf16[512,1536]{1,0:T(8,128)(2,1)} %param.30) | copy-start | bytes 4718596
  7.2 414.1 %all-gather.9.cloned.1.call-start = ((), (), s32[]{:S(2)}) async-start(), calls=%async_computation.11 | async-start | bytes 2801664 | tf_op jit(solution)/shard_map/all_gather | solution.py:218
  7.2 56.9 %collective-permute-start = (bf16[384,6448]{0,1:T(8,128)(2,1)}, bf16[384,6448]{0,1:T(8,128)(2,1)S(1)}, u32[]{:S(2)}, u32[]{:S(2)}) collective-permute-start(bf16[384,6448]{0,1:T(8,128)(2,1)} %param.34), channel_id=1, source_target_pairs={{0,24},{8,0},{16,8},{24,16},{1,25},{9,1},{17,9},{25,17},{2,26},{10... | collective-permute-start | bytes 14856200 | tf_op jit(solution)/shard_map/ppermute | solution.py:188
  71.8 225.6 %collective-permute-start.1 = (bf16[768,6448]{0,1:T(8,128)(2,1)}, bf16[768,6448]{0,1:T(8,128)(2,1)}, u32[]{:S(2)}, u32[]{:S(2)}) collective-permute-start(bf16[768,6448]{0,1:T(8,128)(2,1)} %pad_maximum_fusion), channel_id=1, source_target_pairs={{0,16},{8,24},{16,0},{24,8},{1,17},{9,25},{17,1},{25,9},{2,18},{10... | collective-permute-start | bytes 29712392 | tf_op jit(solution)/shard_map/ppermute | solution.py:188
  288.6 36.1 %copy-start.33 = (f32[1536]{0:T(1024)}, f32[1536]{0:T(1024)S(1)}, u32[]{:S(2)}) copy-start(f32[1536]{0:T(1024)S(1)} %reshape.690) | copy-start | bytes 18436
  289.0 35.7 %copy-start.57 = (f32[512]{0:T(512)}, f32[512]{0:T(512)S(1)}, u32[]{:S(2)}) copy-start(f32[512]{0:T(512)S(1)} %fusion.192) | copy-start | bytes 6148
  324.7 20.2 copy-start.86
  324.7 20.2 copy-start.88
  324.7 20.3 copy-start.28
  324.8 22.9 copy-start.62
  324.8 28.7 %copy-start.72 = (u32[32]{0:T(128)S(1)}, u32[32]{0:T(128)}, u32[]{:S(2)}) copy-start(u32[32]{0:T(128)} %constant.441) | copy-start | bytes 388
  324.8 30.0 %copy-start.73 = (bf16[832]{0:T(1024)(128)(2,1)S(1)}, bf16[832]{0:T(1024)(128)(2,1)}, u32[]{:S(2)}) copy-start(bf16[832]{0:T(1024)(128)(2,1)} %param.36) | copy-start | bytes 4996
  324.8 39.4 %copy-start.87 = (bf16[48]{0:T(256)(128)(2,1)S(1)}, bf16[48]{0:T(256)(128)(2,1)}, u32[]{:S(2)}) copy-start(bf16[48]{0:T(256)(128)(2,1)} %param.39) | copy-start | bytes 292
  344.1 576.3 %all-gather.11.cloned.1.call-start = ((), (), s32[]{:S(2)}) async-start(), calls=%async_computation.12 | async-start | bytes 11796480 | tf_op jit(solution)/shard_map/all_gather | solution.py:199
  345.0 80.4 %copy-start.76 = (f32[48]{0:T(128)}, f32[48]{0:T(128)S(1)}, u32[]{:S(2)}) copy-start(f32[48]{0:T(128)S(1)} %convert_element_type.243) | copy-start | bytes 580
  345.0 80.4 %copy-start.78 = (f32[48]{0:T(128)}, f32[48]{0:T(128)S(1)}, u32[]{:S(2)}) copy-start(f32[48]{0:T(128)S(1)} %convert_exponential_fusion) | copy-start | bytes 580
  346.4 87.6 %copy-start.31 = (f32[4096]{0:T(1024)}, f32[4096]{0:T(1024)S(1)}, u32[]{:S(2)}) copy-start(f32[4096]{0:T(1024)S(1)} %get-tuple-element.1069) | copy-start | bytes 49156
  363.6 81.3 %copy-start.37 = (f32[1,256]{1,0:T(1,128)}, f32[1,256]{1,0:T(1,128)S(1)}, u32[]{:S(2)}) copy-start(f32[1,256]{1,0:T(1,128)S(1)} %get-tuple-element.1109) | copy-start | bytes 3076
  363.6 81.3 %copy-start.39 = (f32[1,256]{1,0:T(1,128)}, f32[1,256]{1,0:T(1,128)S(1)}, u32[]{:S(2)}) copy-start(f32[1,256]{1,0:T(1,128)S(1)} %get-tuple-element.1110) | copy-start | bytes 3076
  363.6 81.4 %copy-start.41 = (f32[1,256]{1,0:T(1,128)}, f32[1,256]{1,0:T(1,128)S(1)}, u32[]{:S(2)}) copy-start(f32[1,256]{1,0:T(1,128)S(1)} %get-tuple-element.1111) | copy-start | bytes 3076
  368.7 95.6 %all-to-all-start = ((bf16[512,8,384]{0,2,1:T(8,128)(2,1)}), bf16[512,8,384]{0,2,1:T(8,128)(2,1)S(1)}, u32[]{:S(2)}, u32[]{:S(2)}) async-start(bf16[512,8,384]{0,2,1:T(8,128)(2,1)} %bitcast.460), calls=%async_computation | async-start | bytes 6291456 | tf_op jit(solution)/shard_map/all_to_all | solution.py:217
  422.9 21.2 collective-permute-start.2
  438.8 11.1 copy-start.4
  469.4 25.1 %copy-start.6 = (bf16[8,512,384]{2,1,0:T(8,128)(2,1)}, bf16[8,512,384]{2,1,0:T(8,128)(2,1)S(1)}, u32[]{:S(2)}) copy-start(bf16[8,512,384]{2,1,0:T(8,128)(2,1)S(1)} %copy.132) | copy-start | bytes 9437188
  469.5 5.2 collective-permute-start.3
  497.8 316.8 %copy-start.70 = (f32[384]{0:T(512)S(1)}, f32[384]{0:T(512)}, u32[]{:S(2)}) copy-start(f32[384]{0:T(512)} %convolution_reduce_fusion) | copy-start | bytes 4612
  827.4 15.9 copy-start.74
  830.3 84.3 %all-to-all-start.1 = ((bf16[8,512,384]{1,2,0:T(8,128)(2,1)}), bf16[8,512,384]{1,2,0:T(8,128)(2,1)S(1)}, u32[]{:S(2)}, u32[]{:S(2)}) async-start(bf16[8,512,384]{1,2,0:T(8,128)(2,1)} %copy.135), calls=%async_computation.1 | async-start | bytes 6291456 | tf_op jit(solution)/shard_map/all_to_all | solution.py:251
  920.4 12.7 copy-start.12
  920.4 12.7 copy-start.60
  940.8 74.6 %all-to-all-start.2 = ((bf16[512,8,384]{0,2,1:T(8,128)(2,1)}), bf16[512,8,384]{0,2,1:T(8,128)(2,1)S(1)}, u32[]{:S(2)}, u32[]{:S(2)}) async-start(bf16[512,8,384]{0,2,1:T(8,128)(2,1)} %bitcast.462), calls=%async_computation.2 | async-start | bytes 6291456 | tf_op jit(solution)/shard_map/all_to_all | solution.py:270
  944.5 887.4 %reduce-scatter.15.cloned.1.call-start = ((), (), s32[]{:S(2)}) async-start(), calls=%async_computation.13 | async-start | bytes 2801664 | tf_op jit(solution)/shard_map/reduce_scatter | solution.py:302
  1031.3 10.4 copy-start.2
  1609.4 13.2 copy-start.16
  1612.4 10.2 copy-start.19
  1629.6 19.8 slice-start
  1636.4 11.0 copy-start
  1636.4 13.0 slice-start.1
  1649.5 25.9 %copy-start.59 = (f32[384]{0:T(512)S(1)}, f32[384]{0:T(512)}, u32[]{:S(2)}) copy-start(f32[384]{0:T(512)} %multiply_reduce_fusion.15) | copy-start | bytes 4612
  1649.5 27.2 %copy-start.26 = (f32[1,7,32,128]{3,2,1,0:T(8,128)S(1)}, f32[1,7,32,128]{3,2,1,0:T(8,128)}, u32[]{:S(2)}) copy-start(f32[1,7,32,128]{3,2,1,0:T(8,128)} %copy-done.25) | copy-start | bytes 344068
  1649.5 27.2 %copy-start.32 = (f32[4096]{0:T(1024)S(1)}, f32[4096]{0:T(1024)}, u32[]{:S(2)}) copy-start(f32[4096]{0:T(1024)} %copy-done.31) | copy-start | bytes 49156
  1682.4 16.4 copy-start.30
  1682.4 20.2 copy-start.77
  1682.4 20.2 copy-start.79
  1691.7 13.9 copy-start.17
  1697.5 10.2 collective-permute-start.5
  1711.7 199.4 %reduce-scatter.19.cloned.1.call-start = ((), (), s32[]{:S(2)}) async-start(), calls=%async_computation.15 | async-start | bytes 11796480 | tf_op jit(solution)/shard_map/reduce_scatter | solution.py:347
  1728.5 9.2 collective-permute-start.4
  1739.1 92.9 %copy-start.23 = (bf16[512,1536]{1,0:T(8,128)(2,1)S(1)}, bf16[512,1536]{1,0:T(8,128)(2,1)}, u32[]{:S(2)}) copy-start(bf16[512,1536]{1,0:T(8,128)(2,1)} %param.30) | copy-start | bytes 4718596
  1739.1 92.9 %copy-start.34 = (f32[1536]{0:T(1024)S(1)}, f32[1536]{0:T(1024)}, u32[]{:S(2)}) copy-start(f32[1536]{0:T(1024)} %copy-done.33) | copy-start | bytes 18436
  1739.1 92.9 %copy-start.58 = (f32[512]{0:T(512)S(1)}, f32[512]{0:T(512)}, u32[]{:S(2)}) copy-start(f32[512]{0:T(512)} %copy-done.57) | copy-start | bytes 6148
  1743.9 88.1 %all-to-all-start.3 = ((bf16[8,512,384]{1,2,0:T(8,128)(2,1)}), bf16[8,512,384]{1,2,0:T(8,128)(2,1)}, u32[]{:S(2)}, u32[]{:S(2)}) async-start(bf16[8,512,384]{1,2,0:T(8,128)(2,1)} %copy.141), calls=%async_computation.3 | async-start | bytes 6291456 | tf_op jit(solution)/shard_map/all_to_all | solution.py:299
  1748.3 312.5 %reduce-scatter.23.cloned.1.call-start = ((), (), s32[]{:S(2)}) async-start(), calls=%async_computation.17 | async-start | bytes 25067520
  1874.8 188.0 %copy-start.90 = (u32[32]{0:T(128)S(1)}, u32[32]{0:T(128)}, u32[]{:S(2)}) copy-start(u32[32]{0:T(128)} %constant.451) | copy-start | bytes 388
  1874.8 212.7 %reduce-scatter.27.cloned.1.call-start = ((), (), s32[]{:S(2)}) async-start(), calls=%async_computation.19 | async-start | bytes 1064960
  1876.9 243.4 %reduce-scatter.17.cloned.1.call-start = ((), (), s32[]{:S(2)}) async-start(), calls=%async_computation.14 | async-start | bytes 20480 | tf_op jit(solution)/shard_map/reduce_scatter | solution.py:350
  1878.0 304.9 %reduce-scatter.21.cloned.1.call-start = ((), (), s32[]{:S(2)}) async-start(), calls=%async_computation.16 | async-start | bytes 2654208 | tf_op jit(solution)/shard_map/reduce_scatter | solution.py:370
  1911.0 374.4 %reduce-scatter.25.cloned.1.call-start = ((), (), s32[]{:S(2)}) async-start(), calls=%async_computation.18 | async-start | bytes 5640192
  2065.3 11.4 copy-start.64
  2065.3 11.6 copy-start.82
  2088.5 21.3 copy-start.63
  2088.5 73.2 %copy-start.36 = (f32[512]{0:T(512)S(1)}, f32[512]{0:T(512)}, u32[]{:S(2)}) copy-start(f32[512]{0:T(512)} %copy-done.35) | copy-start | bytes 6148
  2088.5 73.3 %copy-start.24 = (bf16[512,1536]{1,0:T(8,128)(2,1)S(1)}, bf16[512,1536]{1,0:T(8,128)(2,1)}, u32[]{:S(2)}) copy-start(bf16[512,1536]{1,0:T(8,128)(2,1)} %param.31) | copy-start | bytes 4718596
  (50 other events, 192.5 us)
Sparse Core Ops, SparseCore 0:
  344.3 76.9 all-gather.8
  422.8 75.6 all-gather.10
  1711.8 120.1 reduce-scatter.14
  1834.6 76.3 reduce-scatter.18
  1913.6 147.1 reduce-scatter.22
  2063.8 23.6 reduce-scatter.26
  2090.6 19.2 reduce-scatter.16
  2113.4 69.3 reduce-scatter.20
  2186.5 98.9 reduce-scatter.24
